TPU v7x, 256 devices: a whole 4x4x8 slice. The times are simulated.
256 devices in a mesh: env: 4 (over x_lo, core), tm: 64 (over x_hi, z, y).
Axes of the slice: x: 4 (x_hi: 2, x_lo: 2; x = x_hi * 2 + x_lo), y: 4, z: 8, core: 2. Of those that a mesh axis runs over, the one named last changes fastest.
Arguments:
- hidden: bfloat16 [4, 64, 256, 1024], P('env', 'tm'), may hold values from -6 to 6
- done_step: int32 [4, 64], P('env', 'tm'), may hold values from 0 to 255
- alive: int32 [4, 64, 256], P('env', None, 'tm'), may hold values 0 or 1
- targets: float32 [4, 64, 256], P('env', None, 'tm'), may hold values from -6 to 6
- gain_t: float32 [1024], replicated, may hold values from 0.25 to 1.75
- w_qkv_t: bfloat16 [1024, 3072], replicated, may hold values from -5 to 5
- w_out_t: bfloat16 [1024, 1024], replicated, may hold values from -0.1875 to 0.1875
- gain_a: float32 [1024], replicated, may hold values from 0.25 to 1.75
- w_qkv_a: bfloat16 [1024, 3072], P('tm'), may hold values from -5 to 5
- w_out_a: bfloat16 [1024, 1024], P('tm'), may hold values from -0.1875 to 0.1875
- w_value: float32 [1024], replicated, may hold values from -0.1875 to 0.1875
Outputs:
- values: float32 [4, 64, 256], P('env', None, 'tm')
- input_grad: bfloat16 [4, 64, 256, 1024], P('env', 'tm')
- qkv_grad: float32 [1024, 3072], P('tm')
- out_grad: float32 [1024, 1024], P('tm')
Inputs may be any that keep to these rules, and one draw needn't show every extreme that they name: `done_step`: the last step of an agent's first episode in the window; later steps form a new episode.
All inputs are finite; a program needn't handle non-finite values. No bound on the sum of `alive` on one device may be relied on, other than what follows from the above.
Results may differ from a plain program's by a relative error of at most 0.02.
Values may be sent and summed in bfloat16 or wider, within the bound.
A program may use at most 128 MiB of HBM per device.

v0:
```python
import math
import jax
import jax.numpy as jnp
from jax import lax
from jax.sharding import PartitionSpec as P

HEADS = 8
HI = lax.Precision.HIGHEST


def norm_scale(rows, gain):
    return rows * lax.rsqrt(jnp.mean(rows * rows, axis=-1, keepdims=True) + 1e-06) * gain


def attend(qkv, allowed, head_count):
    width = qkv.shape[-1] // 3
    size = width // head_count
    shape = qkv.shape[:-1] + (head_count, size)
    queries = qkv[..., :width].reshape(shape)
    key_rows = qkv[..., width : 2 * width].reshape(shape)
    value_rows = qkv[..., 2 * width :].reshape(shape)
    scores = jnp.einsum("qhe,khe->hqk", queries, key_rows, preferred_element_type=jnp.float32)
    scores = jnp.where(allowed[None], scores / math.sqrt(size), -1e30)
    row_max = jnp.max(scores, axis=-1, keepdims=True)
    weights = jnp.exp(scores - row_max)
    probs = (weights / jnp.sum(weights, axis=-1, keepdims=True)).astype(jnp.bfloat16)
    mixed = jnp.einsum("hqk,khe->qhe", probs, value_rows, preferred_element_type=jnp.float32)
    return mixed.reshape(qkv.shape[:-1] + (width,))


def temporal_block(rows, done, gain, w_qkv, w_out, head_count):
    length, width = rows.shape
    rows_f = rows.astype(jnp.float32)
    normed = norm_scale(rows_f, gain).astype(jnp.bfloat16)
    qkv = jnp.dot(normed, w_qkv, preferred_element_type=jnp.float32).astype(jnp.bfloat16)
    positions = jnp.arange(length, dtype=jnp.int32)
    later = positions > done
    allowed = (positions[:, None] >= positions[None, :]) & (later[:, None] == later[None, :])
    mixed = attend(qkv, allowed, head_count).astype(jnp.bfloat16)
    added = jnp.dot(mixed, w_out, preferred_element_type=jnp.float32)
    return (rows_f + added).astype(jnp.bfloat16)


def left_product(left, right):
    return lax.dot_general(
        left, right, (((0,), (0,)), ((), ())), preferred_element_type=jnp.float32
    )


def agent_step(lifted, alive_rows, target_rows, gain, w_qk, z, w_value, head_count):
    agent_count, step_count, width = lifted.shape
    size = width // head_count
    lifted_f = lifted.astype(jnp.float32)
    normed_f, norm_pull = jax.vjp(lambda rows: norm_scale(rows, gain), lifted_f)
    normed = normed_f.astype(jnp.bfloat16).reshape(-1, width)
    qk = jnp.dot(normed, w_qk, preferred_element_type=jnp.float32).astype(jnp.bfloat16)
    qk = qk.reshape(agent_count, step_count, 2, head_count, size)
    q, k = (qk[:, :, 0], qk[:, :, 1])
    s = jnp.dot(normed.astype(jnp.float32), z, precision=HI)
    s = s.reshape(agent_count, step_count, head_count).transpose(1, 2, 0)
    living = alive_rows.T == 1
    allowed = living[:, None, :] | jnp.eye(agent_count, dtype=bool)[None]
    scores = jnp.einsum("qbhe,kbhe->bhqk", q, k, preferred_element_type=jnp.float32)
    scores = jnp.where(allowed[:, None], scores / math.sqrt(size), -1e30)
    weights = jnp.exp(scores - jnp.max(scores, axis=-1, keepdims=True))
    probs = weights / jnp.sum(weights, axis=-1, keepdims=True)
    pv = jnp.sum(probs * s[:, :, None, :], axis=-1)
    predicted = jnp.sum(lifted_f * w_value, axis=-1) + jnp.sum(pv, axis=1).T
    err = 32.0 * alive_rows.astype(jnp.float32) * (predicted - target_rows)
    weighted = probs * err.T[:, None, :, None]
    t = jnp.sum(weighted, axis=2)
    ds = weighted * (s[:, :, None, :] - pv[..., None]) * (1.0 / math.sqrt(size))
    ds = ds.astype(jnp.bfloat16)
    dq = jnp.einsum("bhqk,kbhe->qbhe", ds, k, preferred_element_type=jnp.float32)
    dk = jnp.einsum("bhqk,qbhe->kbhe", ds, q, preferred_element_type=jnp.float32)
    dqk = jnp.stack([dq, dk], axis=2).astype(jnp.bfloat16).reshape(-1, 2 * width)
    t = t.transpose(2, 0, 1).reshape(-1, head_count)
    grad_normed = jnp.dot(dqk, w_qk.T, preferred_element_type=jnp.float32)
    grad_normed = grad_normed + jnp.dot(t, z.T, precision=HI)
    grad_top = err[..., None] * w_value
    grad_lifted = grad_top + norm_pull(grad_normed.reshape(agent_count, step_count, width))[0]
    return (predicted, grad_lifted.astype(jnp.bfloat16), normed, dqk, t)


def per_device(
    hidden, done_step, alive, targets, gain_t, w_qkv_t, w_out_t, gain_a, w_qkv_a, w_out_a, w_value
):
    width = hidden.shape[-1]
    size = width // HEADS
    local_rows = hidden[0, 0]
    done = done_step[0, 0]
    v = lax.all_gather(
        jnp.sum(w_out_a.astype(jnp.float32) * w_value, axis=1), "tm", axis=0, tiled=True
    )
    w_v = w_qkv_a[:, 2 * width :].astype(jnp.float32)
    z = jnp.sum((w_v * v).reshape(-1, HEADS, size), axis=-1)
    z = lax.all_gather(z, "tm", axis=0, tiled=True)
    w_qk = lax.all_gather(w_qkv_a[:, : 2 * width], "tm", axis=0, tiled=True)
    first, pull = jax.vjp(
        lambda rows: temporal_block(rows, done, gain_t, w_qkv_t, w_out_t, HEADS), local_rows
    )
    lifted = lax.all_to_all(first[None], "tm", split_axis=1, concat_axis=0, tiled=True)
    predicted, grad_lifted, normed, dqk, t = agent_step(
        lifted, alive[0], targets[0], gain_a, w_qk, z, w_value, HEADS
    )
    returned = lax.all_to_all(grad_lifted, "tm", split_axis=0, concat_axis=1, tiled=True)
    terms = left_product(normed, dqk).astype(jnp.bfloat16)
    u_terms = lax.dot_general(normed.astype(jnp.float32), t, (((0,), (0,)), ((), ())), precision=HI)
    summed = lax.psum_scatter(terms, "tm", scatter_dimension=0, tiled=True)
    qk_grad = lax.psum(summed, "env").astype(jnp.float32)
    u_mine = lax.psum(u_terms, ("env", "tm"))
    u_mine = lax.dynamic_slice_in_dim(u_mine, lax.axis_index("tm") * w_v.shape[0], w_v.shape[0], 0)
    u_wide = jnp.repeat(u_mine, size, axis=1)
    v_grad = u_wide * v
    mixed_err = lax.psum(jnp.sum(u_wide * w_v, axis=0), "tm")
    mixed_err = lax.dynamic_slice_in_dim(
        mixed_err, lax.axis_index("tm") * w_out_a.shape[0], w_out_a.shape[0], 0
    )
    out_grad = mixed_err[:, None] * w_value
    qkv_grad = jnp.concatenate([qk_grad, v_grad], axis=1)
    input_grad = pull(returned[0])[0]
    return (predicted[None], input_grad[None, None], qkv_grad, out_grad)


def solution(mesh):
    in_specs = (
        P("env", "tm", None, None),
        P("env", "tm"),
        P("env", None, "tm"),
        P("env", None, "tm"),
        P(),
        P(),
        P(),
        P(),
        P("tm", None),
        P("tm", None),
        P(),
    )
    out_specs = (P("env", None, "tm"), P("env", "tm", None, None), P("tm", None), P("tm", None))
    return jax.shard_map(
        per_device, mesh=mesh, in_specs=in_specs, out_specs=out_specs, check_vma=False
    )
```

profile of v0, /device:TPU:1, one launch (start us, length us, event | category | flops | bytes accessed | tf_op | source)
XLA Modules:
  0.0 856.8 jit_solution(7488116643575696525)
XLA Ops:
  11.3 4.9 convolution_convert_fusion
  18.7 2.2 copy.97
  27.5 4.5 reduce.4
  34.2 15.1 %all-to-all-start = ((bf16[64,2,2048]{2,1,0:T(2,128)(2,1)}), bf16[64,2,2048]{2,1,0:T(2,128)(2,1)S(1)}, u32[]{:S(2)}, u32[]{:S(2)}) async-start(bf16[64,2,2048]{2,1,0:T(2,128)(2,1)} %reshape.279), calls=%async_computation | async-start | bytes 1048576 | tf_op jit(solution)/shard_map/all_to_all | solution.py:102
  51.0 156.9 %all-reduce.3 = f32[1024]{0:T(1024)S(1)} all-reduce(f32[1024]{0:T(1024)S(1)} %dynamic-update-slice), channel_id=1, replica_groups=mesh['env'=4,'tm'=64] {'tm'}, use_global_device_ids=true, to_apply=%add.3 | all-reduce | flops 1024 | bytes 8192
  208.9 148.0 %all-gather = f32[64,16,8]{1,2,0:T(8,128)S(1)} all-gather(f32[1,16,8]{1,2,0:T(8,128)S(1)} %bitcast.169), channel_id=1, replica_groups=mesh['env'=4,'tm'=64] {'tm'}, dimensions={0}, use_global_device_ids=true | all-gather | bytes 33280 | tf_op jit(solution)/shard_map/all_gather | solution.py:97
  367.1 3.5 fusion.16
  371.9 3.5 multiply_reduce_fusion.2
  376.7 3.3 convolution_bitcast_fusion
  380.0 3.4 convolution_bitcast_fusion.1
  386.4 2.3 convert_element_type.173
  388.7 4.6 convolution_convert_fusion.1
  395.8 3.8 fusion.115
  401.8 2.6 reshape.260
  404.4 2.8 fusion.47
  407.2 4.9 all-to-all-start.1
  413.6 132.2 %psum.22 = f32[1024,8]{0,1:T(8,128)S(1)} all-reduce(f32[1024,8]{0,1:T(8,128)S(1)} %convolution_bitcast_fusion.2), channel_id=1, replica_groups=mesh['env'=4,'tm'=64] {'env','tm'}, use_global_device_ids=true, to_apply=%region_19.20 | all-reduce | flops 8192 | bytes 65536 | tf_op jit(solution)/shard_map/psum | solution.py:111
  546.8 156.0 %psum.23 = f32[1024]{0:T(1024)S(1)} all-reduce(f32[1024]{0:T(1024)S(1)} %get-tuple-element.19), channel_id=1, replica_groups=mesh['env'=4,'tm'=64] {'tm'}, use_global_device_ids=true, to_apply=%region_21.22 | all-reduce | flops 1024 | bytes 8192 | tf_op jit(solution)/shard_map/psum | solution.py:115
  704.6 2.6 convolution_convert_fusion.5
  708.5 2.3 fusion.6
  716.0 2.9 fusion.52
  718.9 45.1 %reduce-scatter.2.cloned.1.call-done = bf16[16,2048]{1,0:T(8,128)(2,1)} async-done(((bf16[1024,2048]{1,0:T(8,128)(2,1)}), bf16[16,2048]{1,0:T(8,128)(2,1)}) %reduce-scatter.2.cloned.1.call-update) | async-done | bytes 65552 | tf_op jit(solution)/shard_map/reduce_scatter | solution.py:109
  764.1 2.3 fusion.67
  766.4 82.4 %all-reduce.6.cloned.1.call-done = bf16[16,2048]{1,0:T(8,128)(2,1)} async-done(((bf16[16,2048]{1,0:T(8,128)(2,1)}), bf16[16,2048]{1,0:T(8,128)(2,1)}) %all-reduce.6.cloned.1.call-update) | async-done | bytes 65552 | tf_op jit(solution)/shard_map/psum | solution.py:110
  (147 shorter events, 49.0 us)
Async XLA Ops:
  7.2 18.2 %copy-start = (bf16[1024,1024]{1,0:T(8,128)(2,1)S(1)}, bf16[1024,1024]{1,0:T(8,128)(2,1)}, u32[]{:S(2)}) copy-start(bf16[1024,1024]{1,0:T(8,128)(2,1)} %param.17) | copy-start | bytes 6291460
  7.2 359.9 %all-gather.3.cloned.1.call-start = ((), (), s32[]{:S(2)}) async-start(), calls=%async_computation.3 | async-start | bytes 4259840 | tf_op jit(solution)/shard_map/all_gather | solution.py:98
  11.3 4.9 copy-start.28
  17.2 6.8 copy-start.9
  18.7 3.9 copy-start.11
  26.9 22.4 %copy-start.31 = (u32[256]{0:T(256)S(1)}, u32[256]{0:T(256)}, u32[]{:S(2)}) copy-start(u32[256]{0:T(256)} %constant.61) | copy-start | bytes 3076
  26.9 23.7 %copy-start.18 = (f32[1024]{0:T(1024)S(1)}, f32[1024]{0:T(1024)}, u32[]{:S(2)}) copy-start(f32[1024]{0:T(1024)} %param.21) | copy-start | bytes 12292
  27.0 23.7 %copy-start.21 = (bf16[16,1024]{1,0:T(8,128)(2,1)S(1)}, bf16[16,1024]{1,0:T(8,128)(2,1)}, u32[]{:S(2)}) copy-start(bf16[16,1024]{1,0:T(8,128)(2,1)} %param.20) | copy-start | bytes 98308
  32.0 325.1 %copy-start.27 = (s32[1,64,4]{1,2,0:T(4,128)S(1)}, s32[1,64,4]{1,2,0:T(4,128)}, u32[]{:S(2)}) copy-start(s32[1,64,4]{1,2,0:T(4,128)} %param.13) | copy-start | bytes 3076
  34.2 323.7 %all-to-all-start = ((bf16[64,2,2048]{2,1,0:T(2,128)(2,1)}), bf16[64,2,2048]{2,1,0:T(2,128)(2,1)S(1)}, u32[]{:S(2)}, u32[]{:S(2)}) async-start(bf16[64,2,2048]{2,1,0:T(2,128)(2,1)} %reshape.279), calls=%async_computation | async-start | bytes 1048576 | tf_op jit(solution)/shard_map/all_to_all | solution.py:102
  49.3 714.7 %reduce-scatter.2.cloned.1.call-start = ((), (), s32[]{:S(2)}) async-start(), calls=%async_computation.4 | async-start | bytes 4259840 | tf_op jit(solution)/shard_map/reduce_scatter | solution.py:109
  207.9 149.2 %copy-start.19 = (f32[1024]{0:T(1024)}, f32[1024]{0:T(1024)S(1)}, u32[]{:S(2)}) copy-start(f32[1024]{0:T(1024)S(1)} %all-reduce.3) | copy-start | bytes 12292
  357.9 5.6 copy-start.15
  361.3 9.4 %copy-start.23 = (f32[256]{0:T(256)}, f32[256]{0:T(256)S(1)}, u32[]{:S(2)}) copy-start(f32[256]{0:T(256)S(1)} %get-tuple-element.24) | copy-start | bytes 3076
  384.8 4.0 copy-start.24
  401.7 2.7 copy-start.5
  404.4 7.7 copy-start.17
  404.4 141.6 %copy-start.20 = (f32[1024]{0:T(1024)S(1)}, f32[1024]{0:T(1024)}, u32[]{:S(2)}) copy-start(f32[1024]{0:T(1024)} %copy-done.19) | copy-start | bytes 12292
  407.2 296.4 %all-to-all-start.1 = ((bf16[64,4,1024]{2,1,0:T(4,128)(2,1)}), bf16[64,4,1024]{2,1,0:T(4,128)(2,1)S(1)}, u32[]{:S(2)}, u32[]{:S(2)}) async-start(bf16[64,4,1024]{2,1,0:T(4,128)(2,1)} %fusion.47), calls=%async_computation.1 | async-start | bytes 1048576 | tf_op jit(solution)/shard_map/all_to_all | solution.py:106
  412.0 436.7 %all-reduce.6.cloned.1.call-start = ((), (), s32[]{:S(2)}) async-start(), calls=%async_computation.5 | async-start | bytes 131072 | tf_op jit(solution)/shard_map/psum | solution.py:110
  704.6 3.9 copy-start.10
  716.0 2.9 copy-start.26
  716.0 48.0 %copy-start.14 = (bf16[256,1024]{1,0:T(8,128)(2,1)S(1)}, bf16[256,1024]{1,0:T(8,128)(2,1)}, u32[]{:S(2)}) copy-start(bf16[256,1024]{1,0:T(8,128)(2,1)} %squeeze.21) | copy-start | bytes 1572868
  716.0 48.0 %copy-start.29 = (f32[256]{0:T(256)S(1)}, f32[256]{0:T(256)}, u32[]{:S(2)}) copy-start(f32[256]{0:T(256)} %copy-done.28) | copy-start | bytes 3076
  (15 other events, 24.0 us)
Sparse Core Ops, SparseCore 0:
  12.1 128.8 all-gather.2
  393.4 370.5 reduce-scatter.1
  766.8 81.8 all-reduce.5
where the time goes:
time: 858 us; the launch traced here: 857 us
  blocking collectives  593 us (69%)
  waiting for transfers between devices  128 us (15%)
  matrix products  45.3 us (5%)
  local copies, waits for them, and re-layouts  30.5 us (4%)
  other arithmetic  24.6 us (3%)
  starting transfers between devices  20.1 us (2%)
  between operations  15.7 us (2%)
    unnamed x1, blocking collectives  157 us
    psum x1, blocking collectives, per_device(): mixed_err = lax.psum(jnp.sum(u_wide * w_v, axis=0), 'tm')  156 us
    all_gather x1, blocking collectives, per_device(): z = lax.all_gather(z, 'tm', axis=0, tiled=True)  148 us
    psum x1, blocking collectives, per_device(): u_mine = lax.psum(u_terms, ('env', 'tm'))  132 us
    psum x1, waiting for transfers between devices, per_device(): qk_grad = lax.psum(summed, 'env').astype(jnp.float32)  82.4 us
    reduce_scatter x1, waiting for transfers between devices, per_device(): summed = lax.psum_scatter(terms, 'tm', scatter_dimension=0, tiled=True)  45.1 us
  transfers between devices with their start and end apart: 5, of which 2 were waited for; matrix products, arithmetic and copies ran while one was open for 8% of the time, Pallas kernels for 0%

commit v1 on v0

--- a/solution.py
+++ b/solution.py
@@ -94,7 +94,14 @@
     )
     w_v = w_qkv_a[:, 2 * width :].astype(jnp.float32)
     z = jnp.sum((w_v * v).reshape(-1, HEADS, size), axis=-1)
-    z = lax.all_gather(z, "tm", axis=0, tiled=True)
+
+    def touch_trails_by_axis(q_in, d_out):
+        r_now = jnp.concatenate(
+            lax.all_to_all(jnp.stack([q_in] * lax.axis_size("tm")), "tm", 0, 0), axis=d_out
+        )
+        return r_now
+
+    z = touch_trails_by_axis(z, 0)
     w_qk = lax.all_gather(w_qkv_a[:, : 2 * width], "tm", axis=0, tiled=True)
     first, pull = jax.vjp(
         lambda rows: temporal_block(rows, done, gain_t, w_qkv_t, w_out_t, HEADS), local_rows

time: 858 us -> 711 us (0.83)
  blocking collectives: 593 us -> 423 us
  local copies, waits for them, and re-layouts: 30.5 us -> 40.9 us
    all_gather x1 -> x0, blocking collectives: 148 us -> none  [per_device(): z = lax.all_gather(z, 'tm', axis=0, tiled=True)]
    psum x1, blocking collectives: 132 us -> 107 us  [per_device(): u_mine = lax.psum(u_terms, ('env', 'tm'))]
    all_to_all x1, waiting for transfers between devices: 0.01 us -> 9.59 us  [per_device(): lax.all_to_all(first[None], 'tm', split_axis=1, concat_axis=0, tiled=True)]
  transfers between devices with their start and end apart: 5 -> 6, of which waited for: 2 -> 3; matrix products, arithmetic and copies ran while one was open for 8% -> 12% of each run, Pallas kernels for 0% -> 0%
where the time goes in v1:
time: 711 us; the launch traced here: 709 us
  blocking collectives  423 us (59%)
  waiting for transfers between devices  131 us (18%)
  matrix products  44.7 us (6%)
  local copies, waits for them, and re-layouts  40.9 us (6%)
  other arithmetic  30.2 us (4%)
  starting transfers between devices  23.3 us (3%)
  between operations  15.7 us (2%)
    unnamed x1, blocking collectives  161 us
    psum x1, blocking collectives, per_device(): mixed_err = lax.psum(jnp.sum(u_wide * w_v, axis=0), 'tm')  156 us
    psum x1, blocking collectives, per_device(): u_mine = lax.psum(u_terms, ('env', 'tm'))  107 us
    psum x1, waiting for transfers between devices, per_device(): qk_grad = lax.psum(summed, 'env').astype(jnp.float32)  82.8 us
    reduce_scatter x1, waiting for transfers between devices, per_device(): summed = lax.psum_scatter(terms, 'tm', scatter_dimension=0, tiled=True)  38.9 us
    unnamed x74, local copies, waits for them, and re-layouts  14.4 us
  transfers between devices with their start and end apart: 6, of which 3 were waited for; matrix products, arithmetic and copies ran while one was open for 12% of the time, Pallas kernels for 0%

profile of v1, /device:TPU:1, one launch (start us, length us, event | category | flops | bytes accessed | tf_op | source)
XLA Modules:
  0.0 709.4 jit_solution(1014976466130391429)
XLA Ops:
  11.9 160.8 %all-reduce.3 = f32[1024]{0:T(1024)S(1)} all-reduce(f32[1024]{0:T(1024)S(1)} %dynamic-update-slice), channel_id=1, replica_groups=mesh['env'=4,'tm'=64] {'tm'}, use_global_device_ids=true, to_apply=%add.3 | all-reduce | flops 1024 | bytes 8192
  175.1 4.6 all-to-all-start.1
  181.6 4.9 convolution_convert_fusion
  195.1 5.6 reduce.4
  202.9 12.6 %all-to-all-start = ((bf16[64,2,2048]{2,1,0:T(2,128)(2,1)}), bf16[64,2,2048]{2,1,0:T(2,128)(2,1)}, u32[]{:S(2)}, u32[]{:S(2)}) async-start(bf16[64,2,2048]{2,1,0:T(2,128)(2,1)} %reshape.294), calls=%async_computation | async-start | bytes 1048576 | tf_op jit(solution)/shard_map/all_to_all | solution.py:109
  219.7 9.6 %all-to-all-done = bf16[64,2,2048]{2,1,0:T(2,128)(2,1)} async-done(((bf16[64,2,2048]{2,1,0:T(2,128)(2,1)}), bf16[64,2,2048]{2,1,0:T(2,128)(2,1)}, u32[]{:S(2)}, u32[]{:S(2)}) %all-to-all-start) | async-done | bytes 524320 | tf_op jit(solution)/shard_map/all_to_all | solution.py:109
  229.3 4.4 reshape.295
  233.8 2.9 fusion.39
  245.3 3.7 fusion.16
  250.4 3.0 multiply_reduce_fusion.2
  254.0 3.2 convolution_bitcast_fusion
  257.2 3.5 convolution_bitcast_fusion.1
  266.0 4.7 convolution_convert_fusion.1
  276.4 3.8 fusion.113
  282.5 2.5 reshape.277
  285.1 3.4 multiply_convert_fusion
  288.4 5.8 all-to-all-start.2
  295.7 106.8 %psum.22 = f32[1024,8]{0,1:T(8,128)S(1)} all-reduce(f32[1024,8]{0,1:T(8,128)S(1)} %convolution_bitcast_fusion.2), channel_id=1, replica_groups=mesh['env'=4,'tm'=64] {'env','tm'}, use_global_device_ids=true, to_apply=%region_19.20 | all-reduce | flops 8192 | bytes 65536 | tf_op jit(solution)/shard_map/psum | solution.py:118
  403.5 155.7 %psum.23 = f32[1024]{0:T(1024)S(1)} all-reduce(f32[1024]{0:T(1024)S(1)} %get-tuple-element.21), channel_id=1, replica_groups=mesh['env'=4,'tm'=64] {'tm'}, use_global_device_ids=true, to_apply=%region_21.22 | all-reduce | flops 1024 | bytes 8192 | tf_op jit(solution)/shard_map/psum | solution.py:122
  562.0 2.6 convolution_convert_fusion.5
  566.7 2.7 fusion.6
  574.3 2.9 fusion.52
  577.2 38.9 %reduce-scatter.2.cloned.1.call-done = bf16[16,2048]{1,0:T(8,128)(2,1)} async-done(((bf16[1024,2048]{1,0:T(8,128)(2,1)}), bf16[16,2048]{1,0:T(8,128)(2,1)}) %reduce-scatter.2.cloned.1.call-update) | async-done | bytes 65552 | tf_op jit(solution)/shard_map/reduce_scatter | solution.py:116
  618.5 82.8 %all-reduce.6.cloned.1.call-done = bf16[16,2048]{1,0:T(8,128)(2,1)} async-done(((bf16[16,2048]{1,0:T(8,128)(2,1)}), bf16[16,2048]{1,0:T(8,128)(2,1)}) %all-reduce.6.cloned.1.call-update) | async-done | bytes 65552 | tf_op jit(solution)/shard_map/psum | solution.py:117
  (147 shorter events, 62.5 us)
Async XLA Ops:
  7.2 184.9 %copy-start = (bf16[1024,1024]{1,0:T(8,128)(2,1)S(1)}, bf16[1024,1024]{1,0:T(8,128)(2,1)}, u32[]{:S(2)}) copy-start(bf16[1024,1024]{1,0:T(8,128)(2,1)} %param.17) | copy-start | bytes 6291460
  7.2 238.1 %all-gather.2.cloned.1.call-start = ((), (), s32[]{:S(2)}) async-start(), calls=%async_computation.4 | async-start | bytes 4259840 | tf_op jit(solution)/shard_map/all_gather | solution.py:105
  175.1 27.8 %all-to-all-start.1 = ((f32[64,1,128]{2,1,0:T(1,128)}), f32[64,1,128]{2,1,0:T(1,128)S(1)}, u32[]{:S(2)}, u32[]{:S(2)}) async-start(f32[64,1,128]{2,1,0:T(1,128)} %reshape.296), calls=%async_computation.1 | async-start | bytes 65536 | tf_op jit(solution)/shard_map/all_to_all | solution.py:100
  181.6 4.9 copy-start.20
  181.6 4.9 copy-start.25
  194.6 21.1 %copy-start.22 = (s32[1,64,4]{1,2,0:T(4,128)S(1)}, s32[1,64,4]{1,2,0:T(4,128)}, u32[]{:S(2)}) copy-start(s32[1,64,4]{1,2,0:T(4,128)} %param.13) | copy-start | bytes 3076
  202.8 30.9 %copy-start.13 = (f32[1024]{0:T(1024)S(1)}, f32[1024]{0:T(1024)}, u32[]{:S(2)}) copy-start(f32[1024]{0:T(1024)} %param.21) | copy-start | bytes 12292
  202.9 26.5 %all-to-all-start = ((bf16[64,2,2048]{2,1,0:T(2,128)(2,1)}), bf16[64,2,2048]{2,1,0:T(2,128)(2,1)}, u32[]{:S(2)}, u32[]{:S(2)}) async-start(bf16[64,2,2048]{2,1,0:T(2,128)(2,1)} %reshape.294), calls=%async_computation | async-start | bytes 1048576 | tf_op jit(solution)/shard_map/all_to_all | solution.py:109
  215.5 400.6 %reduce-scatter.2.cloned.1.call-start = ((), (), s32[]{:S(2)}) async-start(), calls=%async_computation.5 | async-start | bytes 4259840 | tf_op jit(solution)/shard_map/reduce_scatter | solution.py:116
  238.1 7.2 %copy-start.15 = (f32[1024]{0:T(1024)S(1)}, f32[1024]{0:T(1024)}, u32[]{:S(2)}) copy-start(f32[1024]{0:T(1024)} %param.18) | copy-start | bytes 12292
  250.4 3.0 copy-start.23
  250.4 3.0 copy-start.24
  250.4 3.0 copy-start.27
  254.0 6.7 copy-start.19
  276.4 3.9 copy-start.3
  276.4 3.9 copy-start.16
  280.3 4.7 copy-start.14
  285.1 117.7 %copy-start.18 = (f32[1024]{0:T(1024)S(1)}, f32[1024]{0:T(1024)}, u32[]{:S(2)}) copy-start(f32[1024]{0:T(1024)} %copy-done.17) | copy-start | bytes 12292
  288.4 271.6 %all-to-all-start.2 = ((bf16[64,4,1024]{2,1,0:T(4,128)(2,1)}), bf16[64,4,1024]{2,1,0:T(4,128)(2,1)}, u32[]{:S(2)}, u32[]{:S(2)}) async-start(bf16[64,4,1024]{2,1,0:T(4,128)(2,1)} %get-tuple-element.18), calls=%async_computation.2 | async-start | bytes 1048576 | tf_op jit(solution)/shard_map/all_to_all | solution.py:113
  294.2 407.1 %all-reduce.6.cloned.1.call-start = ((), (), s32[]{:S(2)}) async-start(), calls=%async_computation.6 | async-start | bytes 131072 | tf_op jit(solution)/shard_map/psum | solution.py:117
  566.7 2.7 copy-start.2
  574.3 2.9 copy-start.21
  574.3 41.8 %copy-start.12 = (bf16[256,1024]{1,0:T(8,128)(2,1)S(1)}, bf16[256,1024]{1,0:T(8,128)(2,1)}, u32[]{:S(2)}) copy-start(bf16[256,1024]{1,0:T(8,128)(2,1)} %squeeze.21) | copy-start | bytes 1572868
  574.3 41.8 %copy-start.26 = (f32[256]{0:T(256)S(1)}, f32[256]{0:T(256)}, u32[]{:S(2)}) copy-start(f32[256]{0:T(256)} %copy-done.25) | copy-start | bytes 3076
  (13 other events, 20.1 us)
Sparse Core Ops, SparseCore 0:
  12.1 128.4 all-gather.1
  270.8 345.2 reduce-scatter.1
  618.9 82.3 all-reduce.5
